TPU v7x, 32 devices: a whole 2x2x4 slice. The times are simulated.
32 devices in a mesh: pa: 8 (over y, x, core), pb: 4 (over z).
Axes of the slice: x: 2, y: 2, z: 4, core: 2. Of those that a mesh axis runs over, the one named last changes fastest.
Arguments:
- queries: bfloat16 [4096, 1024], P(('pa', 'pb')), may hold values from -900 to 900
- batch_hidden: bfloat16 [512, 1024], P(('pa', 'pb')), may hold values from -6 to 6
- pool_hidden: bfloat16 [16384, 1024], P(('pa', 'pb')), may hold values from -6 to 6
- projection: bfloat16 [1024, 1024], replicated, may hold values from -0.1875 to 0.1875
- hard_ids: int32 [4096, 16], P(('pa', 'pb')), may hold values from 0 to 2047, as said below
- query_group: int32 [4096], P(('pa', 'pb')), may hold values from 0 to 63
- labels: int32 [4096], P(('pa', 'pb')), may hold values from 0 to 63
- group_lists: int32 [64, 64], replicated, may hold values from 0 to 127, as said below
Outputs:
- query_grad: bfloat16 [4096, 1024], P(('pa', 'pb'))
- batch_hidden_grad: bfloat16 [512, 1024], P(('pa', 'pb'))
- pool_hidden_grad: bfloat16 [16384, 1024], P(('pa', 'pb'))
Inputs may be any that keep to these rules, and one draw needn't show every extreme that they name: `hard_ids`: entry k of a query's list lies in [(k % 4) * 512, (k % 4 + 1) * 512); entries may repeat. `group_lists`: each row holds 64 different values.
All inputs are finite; a program needn't handle non-finite values.
Results may differ from a plain program's by a relative error of at most 0.017.
The roundings to bfloat16 on the way count: a program that leaves them out, or rounds other values in their place, can miss the bound.
Values may be sent and summed in bfloat16 or wider, within the bound.
No kernel may reach another device: no remote copies, remote signals or barrier semaphores. Data moves between devices by JAX's collectives and lax.ppermute only.
A program may use at most 128 MiB of HBM per device.

v0:
```python
import math
import jax
import jax.numpy as jnp
from jax import lax
from jax.sharding import PartitionSpec as P

D = 1024


def pick_rows(table, wanted):
    flat = wanted.reshape(-1)
    table_iota = lax.broadcasted_iota(jnp.int32, (flat.shape[0], table.shape[0]), 1)
    selector = (flat[:, None] == table_iota).astype(jnp.bfloat16)
    found = jnp.dot(selector, table, preferred_element_type=jnp.float32).astype(table.dtype)
    return found.reshape(wanted.shape + (table.shape[1],))


def add_rows(wanted, values, count):
    flat = wanted.reshape(-1)
    row_iota = lax.broadcasted_iota(jnp.int32, (count, flat.shape[0]), 0)
    selector = (row_iota == flat[None, :]).astype(jnp.bfloat16)
    return jnp.dot(selector, values.reshape(flat.shape[0], -1), preferred_element_type=jnp.float32)


def shards(
    queries, batch_hidden, pool_hidden, projection, hard_ids, query_group, labels, group_lists
):
    score_scale = 1.0 / math.sqrt(D)
    owners = lax.axis_size("pb")
    query_rows = queries.shape[0]
    pool_count = pool_hidden.shape[0]
    hard_count = hard_ids.shape[1]
    per_owner = hard_count // owners
    group_size = group_lists.shape[1]
    group_total = group_lists.shape[0]
    dims = (((1,), (1,)), ((), ()))
    batch_proj = jnp.dot(batch_hidden, projection, preferred_element_type=jnp.float32).astype(
        jnp.bfloat16
    )
    pool_proj = jnp.dot(pool_hidden, projection, preferred_element_type=jnp.float32).astype(
        jnp.bfloat16
    )
    column = lax.all_gather(batch_proj, "pa", axis=0, tiled=True)
    column_count = column.shape[0]
    dense = lax.dot_general(queries, column, dims, preferred_element_type=jnp.float32) * score_scale
    group_iota = lax.broadcasted_iota(jnp.int32, (query_rows, group_total, group_size), 1)
    chosen = jnp.sum(
        jnp.where(query_group[:, None, None] == group_iota, group_lists[None, :, :], 0), axis=1
    )
    column_iota = lax.broadcasted_iota(jnp.int32, (query_rows, group_size, column_count), 2)
    member = chosen[:, :, None] == column_iota
    group_scores = jnp.sum(jnp.where(member, dense[:, None, :], 0.0), axis=2)
    owner_of = lax.broadcasted_iota(jnp.int32, hard_ids.shape, 1) % owners
    local_rows = hard_ids - owner_of * pool_count
    requests = (
        local_rows.reshape(query_rows, per_owner, owners)
        .transpose(2, 0, 1)
        .reshape(owners, query_rows * per_owner)
    )
    received = lax.all_to_all(requests, "pb", split_axis=0, concat_axis=0, tiled=True)
    copies = lax.all_gather(queries, "pb", axis=0, tiled=True).reshape(owners, query_rows, D)
    picked = pick_rows(pool_proj, received).reshape(owners, query_rows, per_owner, D)
    owner_scores = (
        jnp.einsum("sid,sijd->sij", copies, picked, preferred_element_type=jnp.float32)
        * score_scale
    )
    returned = lax.all_to_all(owner_scores, "pb", split_axis=0, concat_axis=0, tiled=True)
    hard_scores = returned.transpose(1, 2, 0).reshape(query_rows, hard_count)
    scores = jnp.concatenate([group_scores, hard_scores], axis=1)
    likely = jax.nn.softmax(scores, axis=1)
    positions = lax.broadcasted_iota(jnp.int32, scores.shape, 1)
    target = (positions == labels[:, None]).astype(jnp.float32)
    dscore = (likely - target).astype(jnp.bfloat16)
    grad_group = dscore[:, :group_size]
    grad_hard = dscore[:, group_size:].reshape(query_rows, per_owner, owners).transpose(2, 0, 1)
    dense_grad = jnp.einsum(
        "ic,icr->ir", grad_group, member.astype(jnp.bfloat16), preferred_element_type=jnp.float32
    ).astype(jnp.bfloat16)
    group_term = jnp.dot(dense_grad, column, preferred_element_type=jnp.float32)
    batch_part = (
        lax.dot_general(
            dense_grad, queries, (((0,), (0,)), ((), ())), preferred_element_type=jnp.float32
        )
        * score_scale
    )
    batch_grad = lax.psum_scatter(batch_part, "pa", scatter_dimension=0, tiled=True)
    sent_back = lax.all_to_all(grad_hard, "pb", split_axis=0, concat_axis=0, tiled=True)
    contrib = (
        score_scale
        * sent_back.astype(jnp.float32)[..., None]
        * copies.astype(jnp.float32)[:, :, None, :]
    )
    contrib = contrib.astype(jnp.bfloat16)
    pool_grad = add_rows(received, contrib, pool_count)
    owner_term = jnp.einsum("sij,sijd->sid", sent_back, picked, preferred_element_type=jnp.float32)
    gathered_terms = lax.all_to_all(owner_term, "pb", split_axis=0, concat_axis=0, tiled=True)
    hard_term = jnp.sum(gathered_terms, axis=0)
    query_grad = (score_scale * (group_term + hard_term)).astype(jnp.bfloat16)
    batch_hidden_grad = lax.dot_general(
        batch_grad.astype(jnp.bfloat16), projection, dims, preferred_element_type=jnp.float32
    ).astype(jnp.bfloat16)
    pool_hidden_grad = lax.dot_general(
        pool_grad.astype(jnp.bfloat16), projection, dims, preferred_element_type=jnp.float32
    ).astype(jnp.bfloat16)
    return (query_grad, batch_hidden_grad, pool_hidden_grad)


def solution(mesh):
    return jax.shard_map(
        shards,
        mesh=mesh,
        in_specs=(
            P(("pa", "pb"), None),
            P(("pa", "pb"), None),
            P(("pa", "pb"), None),
            P(),
            P(("pa", "pb"), None),
            P(("pa", "pb")),
            P(("pa", "pb")),
            P(),
        ),
        out_specs=(P(("pa", "pb"), None), P(("pa", "pb"), None), P(("pa", "pb"), None)),
        check_vma=False,
    )
```

profile of v0, /device:TPU:0, one launch (start us, length us, event | category | flops | bytes accessed | tf_op | source)
XLA Modules:
  0.0 145.6 jit_solution(15382826161694779296)
XLA Ops:
  7.2 0.0 copy-start
  7.2 0.0 all-gather.2.cloned.1.call-start
  7.2 0.7 all-gather.2.cloned.1.call-update
  7.9 0.8 multiply_subtract_fusion
  8.7 0.2 copy.23
  8.9 0.8 all_to_all.20
  9.7 6.3 %all-to-all-start = ((s32[4,1,512]{2,1,0:T(1,128)}), s32[4,1,512]{2,1,0:T(1,128)S(1)}, u32[]{:S(2)}, u32[]{:S(2)}) async-start(s32[4,1,512]{2,1,0:T(1,128)} %all_to_all.20), calls=%async_computation | async-start | bytes 16384 | tf_op jit(solution)/shard_map/all_to_all | solution.py:60
  16.0 0.0 copy-done
  16.0 1.1 convolution_convert_fusion.3
  17.1 9.3 %all_gather.6 = bf16[128,1024]{1,0:T(8,128)(2,1)S(1)} all-gather(bf16[16,1024]{1,0:T(8,128)(2,1)S(1)} %convolution_convert_fusion.3), channel_id=1, replica_groups=mesh['pa'=8,'pb'=4] {'pa'}, dimensions={0}, use_global_device_ids=true | all-gather | bytes 294912 | tf_op jit(solution)/shard_map/all_gather | solution.py:43
  26.4 1.2 fusion.13
  27.6 1.4 select_reduce_fusion.1
  29.1 0.1 copy.22
  29.1 0.1 copy.21
  29.3 0.0 all-to-all-done
  29.3 6.6 %fusion.4 = bf16[2048,1024]{1,0:T(8,128)(2,1)} fusion(s32[2048]{0:T(1024)S(1)} %bitcast.47, bf16[512,1024]{1,0:T(8,128)(2,1)} %param.10, bf16[1024,1024]{1,0:T(8,128)(2,1)S(1)} %copy-done), kind=kOutput, calls=%fused_computation.9 | convolution fusion | flops 3224895488 | bytes 7348224 | tf_op jit(solution)/shard_map/dot_general | solution.py:14
  35.8 7.2 %reshape_reshape.3 = bf16[4,128,4,1024]{3,2,1,0:T(4,128)(2,1)} reshape(bf16[2048,1024]{1,0:T(8,128)(2,1)} %fusion.4) | data formatting | bytes 8388608 | tf_op jit(solution)/shard_map/reshape;reshape | solution.py:62
  43.0 0.0 all-gather.2.cloned.1.call-done
  43.0 0.0 copy-start.3
  43.0 6.8 %fusion.8 = f32[4,128,1,4]{3,2,1,0:T(1,128)S(1)} fusion(bf16[4,128,4,1024]{3,2,1,0:T(4,128)(2,1)} %reshape_reshape.3, bf16[4,128,1024,1]{2,1,0,3:T(8,128)(2,1)} %bitcast.37), kind=kOutput, calls=%fused_computation.16 | convolution fusion | flops 4194304 | bytes 5251072 | tf_op jit(solution)/shard_map/sid,sijd->sij/dot_general | solution.py:64
  49.8 0.1 copy.31
  49.9 0.6 bitcast_multiply_fusion
  50.6 5.1 %all-to-all-start.1 = ((f32[4,128,4]{1,2,0:T(4,128)}), f32[4,128,4]{1,2,0:T(4,128)S(1)}, u32[]{:S(2)}, u32[]{:S(2)}) async-start(f32[4,128,4]{1,2,0:T(4,128)} %bitcast_multiply_fusion), calls=%async_computation.1 | async-start | bytes 16384 | tf_op jit(solution)/shard_map/all_to_all | solution.py:67
  55.6 2.6 %select_reduce_fusion = f32[128,64]{1,0:T(8,128)S(1)} fusion(f32[128,128]{1,0:T(8,128)S(1)} %copy.22, s32[128,64]{1,0:T(8,128)S(1)} %copy.21), kind=kLoop, calls=%fused_computation.5 | loop fusion | flops 3137536 | bytes 131072 | tf_op jit(solution)/shard_map/reduce_sum | solution.py:52
  58.2 0.1 reduce_max.20
  58.3 2.9 %all-to-all-done.1 = f32[4,128,4]{1,2,0:T(4,128)S(1)} async-done(((f32[4,128,4]{1,2,0:T(4,128)}), f32[4,128,4]{1,2,0:T(4,128)S(1)}, u32[]{:S(2)}, u32[]{:S(2)}) %all-to-all-start.1) | async-done | bytes 8224 | tf_op jit(solution)/shard_map/all_to_all | solution.py:67
  61.2 0.1 copy.26
  61.4 0.2 fusion.19
  61.6 0.0 copy-done.3
  61.6 0.1 subtract_convert_fusion
  61.7 0.1 slice.9
  61.8 0.1 copy.27
  61.9 7.9 %all_to_all.25 = bf16[4,128,4]{1,2,0:T(4,128)(2,1)S(1)} all-to-all(bf16[4,128,4]{1,2,0:T(4,128)(2,1)S(1)} %copy.28), channel_id=1, replica_groups=mesh['pa'=8,'pb'=4] {'pb'}, dimensions={0} | all-to-all | bytes 8192 | tf_op jit(solution)/shard_map/all_to_all | solution.py:87
  69.8 0.2 copy.34
  70.0 4.5 %fusion.20 = f32[4,128,1,1024]{3,2,1,0:T(1,128)S(1)} fusion(bf16[4,128,4,1]{2,3,1,0:T(2,128)(2,1)S(1)} %copy.34, bf16[4,128,4,1024]{3,2,1,0:T(4,128)(2,1)} %reshape_reshape.3), kind=kOutput, calls=%fused_computation.45 | convolution fusion | flops 4194304 | bytes 6295552 | tf_op jit(solution)/shard_map/sij,sijd->sid/dot_general | solution.py:95
  74.5 0.0 copy-start.2
  74.5 1.8 %copy.41 = f32[4,128,1,1024]{3,1,0,2:T(8,128)} copy(f32[4,128,1,1024]{3,2,1,0:T(1,128)S(1)} %fusion.20) | data formatting | bytes 4194304 | tf_op jit(solution)/shard_map/sij,sijd->sid/dot_general | solution.py:95
  76.3 4.4 %all-to-all-start.3 = ((f32[4,128,1024]{2,1,0:T(8,128)}), f32[4,128,1024]{2,1,0:T(8,128)}, u32[]{:S(2)}, u32[]{:S(2)}) async-start(f32[4,128,1024]{2,1,0:T(8,128)} %bitcast.36), calls=%async_computation.3 | async-start | bytes 4194304 | tf_op jit(solution)/shard_map/all_to_all | solution.py:96
  80.7 0.0 reduce-scatter.2.cloned.1.call-start
  80.8 0.0 copy-done.2
  80.8 5.5 %mul.62 = f32[4,128,4,1024]{3,2,1,0:T(4,128)} broadcast(bf16[4,128,1024]{2,1,0:T(8,128)(2,1)S(1)} %bitcast.38), dimensions={0,1,3} | broadcast | bytes 9437184 | tf_op jit(solution)/shard_map/mul | solution.py:89
  86.3 0.0 copy-start.1
  86.3 10.0 %mul.63 = f32[2048,1024]{1,0:T(8,128)} reshape(f32[4,128,4,1024]{3,2,1,0:T(4,128)} %mul.62) | data formatting | bytes 16777216 | tf_op jit(solution)/shard_map/mul | solution.py:89
  96.3 1.8 %fusion.2 = f32[128,1,128]{2,1,0:T(1,128)S(1)} fusion(s32[128,64]{1,0:T(8,128)S(1)} %copy.21, bf16[128,64,1]{1,0,2:T(8,128)(2,1)S(1)} %slice_bitcast_fusion), kind=kOutput, calls=%fused_computation.7 | convolution fusion | flops 3145728 | bytes 114688 | tf_op jit(solution)/shard_map/ic,icr->ir/dot_general | solution.py:76
  98.1 0.0 copy-done.1
  98.1 1.1 convolution_multiply_fusion
  99.2 0.0 reduce-scatter.2.cloned.1.call-update
  99.3 0.1 copy.29
  99.4 0.2 mul.60
  99.6 7.9 %convolution_convert_fusion = bf16[512,1024]{1,0:T(8,128)(2,1)} fusion(bf16[1024,1024]{1,0:T(8,128)(2,1)S(1)} %copy-done, f32[2048,1024]{1,0:T(8,128)} %mul.63, f32[2048]{0:T(1024)S(1)} %mul.60, s32[2048]{0:T(1024)S(1)} %bitcast.48), kind=kOutput, calls=%fused_computation.19 | convolution fusion | flops 3227516928 | bytes 11550720 | tf_op jit(solution)/shard_map/dot_general | solution.py:102
  107.5 26.5 %reduce-scatter.2.cloned.1.call-done = f32[16,1024]{1,0:T(8,128)} async-done(((f32[128,1024]{1,0:T(8,128)}), f32[16,1024]{1,0:T(8,128)}) %reduce-scatter.2.cloned.1.call-update) | async-done | bytes 65552 | tf_op jit(solution)/shard_map/reduce_scatter | solution.py:86
  133.9 2.1 %convolution_convert_fusion.2 = bf16[16,1024]{1,0:T(8,128)(2,1)} fusion(bf16[1024,1024]{1,0:T(8,128)(2,1)S(1)} %copy-done, f32[16,1024]{1,0:T(8,128)} %reduce-scatter.2.cloned.1.call-done), kind=kOutput, calls=%fused_computation.27 | convolution fusion | flops 33587200 | bytes 2195456 | tf_op jit(solution)/shard_map/dot_general | solution.py:99
  136.1 0.0 all-to-all-done.3
  136.1 1.8 %reduce_sum.39 = f32[128,1024]{1,0:T(8,128)S(1)} reduce(f32[4,128,1024]{2,1,0:T(8,128)} %all-to-all-done.3, f32[]{:T(128)} %constant.11.clone.1), dimensions={0}, to_apply=%region_5.6 | reduce | flops 393216 | bytes 2621444 | tf_op jit(solution)/shard_map/reduce_sum | solution.py:97
  137.9 0.9 fusion.12
  (8 shorter events, 0.1 us)
Async XLA Ops:
  7.2 8.8 %copy-start = (bf16[1024,1024]{1,0:T(8,128)(2,1)S(1)}, bf16[1024,1024]{1,0:T(8,128)(2,1)}, u32[]{:S(2)}) copy-start(bf16[1024,1024]{1,0:T(8,128)(2,1)} %param.11) | copy-start | bytes 6291460
  7.2 35.9 %all-gather.2.cloned.1.call-start = ((), (), s32[]{:S(2)}) async-start(), calls=%async_computation.5 | async-start | bytes 1310720 | tf_op jit(solution)/shard_map/all_gather | solution.py:61
  9.7 19.6 %all-to-all-start = ((s32[4,1,512]{2,1,0:T(1,128)}), s32[4,1,512]{2,1,0:T(1,128)S(1)}, u32[]{:S(2)}, u32[]{:S(2)}) async-start(s32[4,1,512]{2,1,0:T(1,128)} %all_to_all.20), calls=%async_computation | async-start | bytes 16384 | tf_op jit(solution)/shard_map/all_to_all | solution.py:60
  43.0 18.5 %copy-start.3 = (s32[128]{0:T(128)S(1)}, s32[128]{0:T(128)}, u32[]{:S(2)}) copy-start(s32[128]{0:T(128)} %param.14) | copy-start | bytes 1540
  50.6 10.7 %all-to-all-start.1 = ((f32[4,128,4]{1,2,0:T(4,128)}), f32[4,128,4]{1,2,0:T(4,128)S(1)}, u32[]{:S(2)}, u32[]{:S(2)}) async-start(f32[4,128,4]{1,2,0:T(4,128)} %bitcast_multiply_fusion), calls=%async_computation.1 | async-start | bytes 16384 | tf_op jit(solution)/shard_map/all_to_all | solution.py:67
  74.5 6.3 %copy-start.2 = (bf16[512,1024]{1,0:T(8,128)(2,1)S(1)}, bf16[512,1024]{1,0:T(8,128)(2,1)}, u32[]{:S(2)}) copy-start(bf16[512,1024]{1,0:T(8,128)(2,1)} %all-gather.2.cloned.1.call-done) | copy-start | bytes 3145732
  76.3 59.8 %all-to-all-start.3 = ((f32[4,128,1024]{2,1,0:T(8,128)}), f32[4,128,1024]{2,1,0:T(8,128)}, u32[]{:S(2)}, u32[]{:S(2)}) async-start(f32[4,128,1024]{2,1,0:T(8,128)} %bitcast.36), calls=%async_computation.3 | async-start | bytes 4194304 | tf_op jit(solution)/shard_map/all_to_all | solution.py:96
  80.7 53.2 %reduce-scatter.2.cloned.1.call-start = ((), (), s32[]{:S(2)}) async-start(), calls=%async_computation.6 | async-start | bytes 589824 | tf_op jit(solution)/shard_map/reduce_scatter | solution.py:86
  86.3 11.8 %copy-start.1 = (bf16[128,1024]{1,0:T(8,128)(2,1)S(1)}, bf16[128,1024]{1,0:T(8,128)(2,1)}, u32[]{:S(2)}) copy-start(bf16[128,1024]{1,0:T(8,128)(2,1)} %param.8) | copy-start | bytes 786436
Sparse Core Ops, SparseCore 0:
  9.6 30.6 all-gather.1
  99.4 34.5 reduce-scatter.1
where the time goes:
time: 147 us; the launch traced here: 146 us
  matrix products  34 us (23%)
  waiting for transfers between devices  30.1 us (20%)
  local copies, waits for them, and re-layouts  26.5 us (18%)
  blocking collectives  17.2 us (12%)
  starting transfers between devices  16 us (11%)
  between operations  14.2 us (10%)
  other arithmetic  7.67 us (5%)
    reduce_scatter x1, waiting for transfers between devices, shards(): lax.psum_scatter(batch_part, 'pa', scatter_dimension=0, tiled=True)  26.5 us
    mul x4, local copies, waits for them, and re-layouts, shards(): score_scale * sent_back.astype(jnp.float32)[..., None]  15.8 us
    all_gather x1, blocking collectives, shards(): column = lax.all_gather(batch_proj, 'pa', axis=0, tiled=True)  9.29 us
    all_to_all x1, blocking collectives, shards(): lax.all_to_all(grad_hard, 'pb', split_axis=0, concat_axis=0, tiled=True)  7.94 us
    dot_general x1, matrix products, shards(): lax.dot_general(pool_grad.astype(jnp.bfloat16), projection, dims, preferr...  7.86 us
    another operation x1, local copies, waits for them, and re-layouts, shards(): pick_rows(pool_proj, received).reshape(owners, query_rows, per_owner, D)  7.2 us
    dot_general x1, matrix products, shards(): jnp.einsum('sid,sijd->sij', copies, picked, preferred_element_type=jnp.fl...  6.77 us
    dot_general x1, matrix products, pick_rows(): jnp.dot(selector, table, preferred_element_type=jnp.float32)  6.57 us
  transfers between devices with their start and end apart: 5, of which 2 were waited for; matrix products, arithmetic and copies ran while one was open for 34% of the time, Pallas kernels for 0%

commit v1 on v0

--- a/solution.py
+++ b/solution.py
@@ -1,10 +1,41 @@
+import functools
 import math
 import jax
 import jax.numpy as jnp
 from jax import lax
 from jax.sharding import PartitionSpec as P
+from jax.lax import axis_index, axis_size, ppermute
 
 D = 1024
+
+
+def _direct_space(frame, peer_axis):
+    out_arr = axis_size(peer_axis)
+    mat_out = axis_index(peer_axis)
+    plain, o_now, z_new = (out_arr, mat_out, frame.shape[0])
+    arr_now = map(lambda c: (c, (c + 1) % plain), range(plain))
+    pile = list(arr_now)
+    new = range(plain)
+    built = map(lambda c: (c, (c - 1) % plain), new)
+    all_rows = list(built)
+    part_next = jnp.zeros((*frame.shape[:0], plain * z_new, *frame.shape[1:]), frame.dtype)
+    part_next = lax.dynamic_update_slice_in_dim(part_next, frame, o_now * z_new, axis=0)
+    fresh = finding = frame
+    base_arr = plain // 2
+    for dev_j in [*range(1, base_arr + 1)]:
+        fresh = ppermute(fresh, peer_axis, pile)
+        part_next = lax.dynamic_update_slice_in_dim(
+            part_next, fresh, (o_now - dev_j) % plain * z_new, axis=0
+        )
+        if dev_j < plain - base_arr:
+            finding = ppermute(finding, peer_axis, all_rows)
+            part_next = lax.dynamic_update_slice_in_dim(
+                part_next, finding, (o_now + dev_j) % plain * z_new, axis=0
+            )
+    return part_next
+
+
+ports_scan = functools.partial(_direct_space, peer_axis="pa")
 
 
 def pick_rows(table, wanted):
@@ -40,7 +71,7 @@
     pool_proj = jnp.dot(pool_hidden, projection, preferred_element_type=jnp.float32).astype(
         jnp.bfloat16
     )
-    column = lax.all_gather(batch_proj, "pa", axis=0, tiled=True)
+    column = ports_scan(batch_proj)
     column_count = column.shape[0]
     dense = lax.dot_general(queries, column, dims, preferred_element_type=jnp.float32) * score_scale
     group_iota = lax.broadcasted_iota(jnp.int32, (query_rows, group_total, group_size), 1)

time: 147 us -> 157 us (1.068)
  waiting for transfers between devices: 30.1 us -> 40.6 us
  blocking collectives: 17.2 us -> 7.94 us
  starting transfers between devices: 16 us -> 22.4 us
  local copies, waits for them, and re-layouts: 26.5 us -> 29.4 us
    all_gather x1 -> x0, blocking collectives: 9.29 us -> none  [shards(): column = lax.all_gather(batch_proj, 'pa', axis=0, tiled=True)]
    ppermute x0 -> x7, starting transfers between devices: none -> 9.07 us  [the longest x3 8.57 us: _direct_space(): finding = ppermute(finding, peer_axis, all_rows)]
    ppermute x0 -> x7, waiting for transfers between devices: none -> 6.99 us  [the longest x4 6.58 us: _direct_space(): fresh = ppermute(fresh, peer_axis, pile)]
    all_to_all x1, waiting for transfers between devices: 0.01 us -> 3.19 us  [shards(): lax.all_to_all(requests, 'pb', split_axis=0, concat_axis=0, tiled=True)]
    all_to_all x1, starting transfers between devices: 5.09 us -> 3.25 us  [shards(): lax.all_to_all(owner_scores, 'pb', split_axis=0, concat_axis=0, tiled=True)]
  transfers between devices with their start and end apart: 5 -> 12, of which waited for: 2 -> 7; matrix products, arithmetic and copies ran while one was open for 34% -> 32% of each run, Pallas kernels for 0% -> 0%
where the time goes in v1:
time: 157 us; the launch traced here: 155 us
  waiting for transfers between devices  40.6 us (26%)
  matrix products  33 us (21%)
  local copies, waits for them, and re-layouts  29.4 us (19%)
  starting transfers between devices  22.4 us (14%)
  between operations  14.4 us (9%)
  blocking collectives  7.94 us (5%)
  other arithmetic  7.68 us (5%)
    reduce_scatter x1, waiting for transfers between devices, shards(): lax.psum_scatter(batch_part, 'pa', scatter_dimension=0, tiled=True)  26.8 us
    mul x4, local copies, waits for them, and re-layouts, shards(): score_scale * sent_back.astype(jnp.float32)[..., None]  17 us
    ppermute x3, starting transfers between devices, _direct_space(): finding = ppermute(finding, peer_axis, all_rows)  8.57 us
    all_to_all x1, blocking collectives, shards(): lax.all_to_all(grad_hard, 'pb', split_axis=0, concat_axis=0, tiled=True)  7.94 us
    dot_general x1, matrix products, shards(): lax.dot_general(pool_grad.astype(jnp.bfloat16), projection, dims, preferr...  7.86 us
    another operation x1, local copies, waits for them, and re-layouts, shards(): pick_rows(pool_proj, received).reshape(owners, query_rows, per_owner, D)  7.26 us
    dot_general x1, matrix products, shards(): jnp.einsum('sid,sijd->sij', copies, picked, preferred_element_type=jnp.fl...  6.77 us
    dot_general x1, matrix products, pick_rows(): jnp.dot(selector, table, preferred_element_type=jnp.float32)  6.59 us
  transfers between devices with their start and end apart: 12, of which 7 were waited for; matrix products, arithmetic and copies ran while one was open for 32% of the time, Pallas kernels for 0%

profile of v1, /device:TPU:0, one launch (start us, length us, event | category | flops | bytes accessed | tf_op | source)
XLA Modules:
  0.0 155.4 jit_solution(15289292224177315846)
XLA Ops:
  7.2 0.0 copy-start
  7.2 1.5 copy-done
  8.8 1.1 constant_dynamic-update-slice_fusion.7
  9.9 0.5 collective-permute-start
  10.4 2.9 %collective-permute-start.1 = (bf16[16,1024]{1,0:T(8,128)(2,1)S(1)}, bf16[16,1024]{1,0:T(8,128)(2,1)S(1)}, u32[]{:S(2)}, u32[]{:S(2)}) collective-permute-start(bf16[16,1024]{1,0:T(8,128)(2,1)S(1)} %get-tuple-element.4), channel_id=1, source_target_pairs={{0,28},{4,0},{8,4},{12,8},{16,12},{20,16},{24,20},{28,24},{1,29},{... | collective-permute-start | bytes 98312 | tf_op jit(solution)/shard_map/ppermute | solution.py:31
  13.3 0.8 multiply_subtract_fusion
  14.1 0.2 copy.23
  14.2 0.8 all_to_all.20
  15.0 5.6 %all-to-all-start = ((s32[4,1,512]{2,1,0:T(1,128)}), s32[4,1,512]{2,1,0:T(1,128)S(1)}, u32[]{:S(2)}, u32[]{:S(2)}) async-start(s32[4,1,512]{2,1,0:T(1,128)} %all_to_all.20), calls=%async_computation | async-start | bytes 16384 | tf_op jit(solution)/shard_map/all_to_all | solution.py:91
  20.6 0.0 all-gather.2.cloned.1.call-start
  20.6 0.7 all-gather.2.cloned.1.call-update
  21.3 1.4 select_reduce_fusion.1
  22.9 0.1 copy.21
  23.0 3.2 %all-to-all-done = s32[4,1,512]{2,1,0:T(1,128)S(1)} async-done(((s32[4,1,512]{2,1,0:T(1,128)}), s32[4,1,512]{2,1,0:T(1,128)S(1)}, u32[]{:S(2)}, u32[]{:S(2)}) %all-to-all-start) | async-done | bytes 8224 | tf_op jit(solution)/shard_map/all_to_all | solution.py:91
  26.2 6.6 %fusion.4 = bf16[2048,1024]{1,0:T(8,128)(2,1)} fusion(s32[2048]{0:T(1024)S(1)} %bitcast.47, bf16[512,1024]{1,0:T(8,128)(2,1)} %param.10, bf16[1024,1024]{1,0:T(8,128)(2,1)S(1)} %copy-done), kind=kOutput, calls=%fused_computation.9 | convolution fusion | flops 3224895488 | bytes 7348224 | tf_op jit(solution)/shard_map/dot_general | solution.py:45
  32.8 7.3 %reshape_reshape.3 = bf16[4,128,4,1024]{3,2,1,0:T(4,128)(2,1)} reshape(bf16[2048,1024]{1,0:T(8,128)(2,1)} %fusion.4) | data formatting | bytes 8388608 | tf_op jit(solution)/shard_map/reshape;reshape | solution.py:93
  40.1 0.0 collective-permute-done
  40.1 0.0 collective-permute-start.2
  40.1 0.0 collective-permute-done.1
  40.1 2.6 %collective-permute-start.3 = (bf16[16,1024]{1,0:T(8,128)(2,1)S(1)}, bf16[16,1024]{1,0:T(8,128)(2,1)S(1)}, u32[]{:S(2)}, u32[]{:S(2)}) collective-permute-start(bf16[16,1024]{1,0:T(8,128)(2,1)S(1)} %collective-permute-done.1), channel_id=1, source_target_pairs={{0,28},{4,0},{8,4},{12,8},{16,12},{20,16},{24,20},{28,24},{1,29},{... | collective-permute-start | bytes 98312 | tf_op jit(solution)/shard_map/ppermute | solution.py:31
  42.7 1.6 %collective-permute-done.2 = bf16[16,1024]{1,0:T(8,128)(2,1)S(1)} collective-permute-done((bf16[16,1024]{1,0:T(8,128)(2,1)S(1)}, bf16[16,1024]{1,0:T(8,128)(2,1)S(1)}, u32[]{:S(2)}, u32[]{:S(2)}) %collective-permute-start.2) | collective-permute-done | bytes 32800 | tf_op jit(solution)/shard_map/ppermute | solution.py:26
  44.3 0.0 collective-permute-start.4
  44.3 0.0 collective-permute-done.3
  44.3 3.0 %collective-permute-start.5 = (bf16[16,1024]{1,0:T(8,128)(2,1)S(1)}, bf16[16,1024]{1,0:T(8,128)(2,1)S(1)}, u32[]{:S(2)}, u32[]{:S(2)}) collective-permute-start(bf16[16,1024]{1,0:T(8,128)(2,1)S(1)} %collective-permute-done.3), channel_id=1, source_target_pairs={{0,28},{4,0},{8,4},{12,8},{16,12},{20,16},{24,20},{28,24},{1,29},{... | collective-permute-start | bytes 98312 | tf_op jit(solution)/shard_map/ppermute | solution.py:31
  47.4 1.2 collective-permute-done.4
  48.5 0.0 collective-permute-start.6
  48.6 0.4 collective-permute-done.5
  49.0 3.8 %collective-permute-done.6 = bf16[16,1024]{1,0:T(8,128)(2,1)S(1)} collective-permute-done((bf16[16,1024]{1,0:T(8,128)(2,1)S(1)}, bf16[16,1024]{1,0:T(8,128)(2,1)S(1)}, u32[]{:S(2)}, u32[]{:S(2)}) %collective-permute-start.6) | collective-permute-done | bytes 32800 | tf_op jit(solution)/shard_map/ppermute | solution.py:26
  52.8 0.0 copy-done.1
  52.8 0.2 fusion.13
  53.0 0.1 copy.22
  53.1 0.0 all-gather.2.cloned.1.call-done
  53.2 0.0 copy-start.2
  53.2 6.8 %fusion.8 = f32[4,128,1,4]{3,2,1,0:T(1,128)S(1)} fusion(bf16[4,128,4,1024]{3,2,1,0:T(4,128)(2,1)} %reshape_reshape.3, bf16[4,128,1024,1]{2,1,0,3:T(8,128)(2,1)} %bitcast.37), kind=kOutput, calls=%fused_computation.16 | convolution fusion | flops 4194304 | bytes 5251072 | tf_op jit(solution)/shard_map/sid,sijd->sij/dot_general | solution.py:95
  59.9 0.1 copy.31
  60.1 0.6 bitcast_multiply_fusion
  60.7 3.2 %all-to-all-start.1 = ((f32[4,128,4]{1,2,0:T(4,128)}), f32[4,128,4]{1,2,0:T(4,128)S(1)}, u32[]{:S(2)}, u32[]{:S(2)}) async-start(f32[4,128,4]{1,2,0:T(4,128)} %bitcast_multiply_fusion), calls=%async_computation.1 | async-start | bytes 16384 | tf_op jit(solution)/shard_map/all_to_all | solution.py:98
  63.9 2.6 %select_reduce_fusion = f32[128,64]{1,0:T(8,128)S(1)} fusion(f32[128,128]{1,0:T(8,128)S(1)} %copy.22, s32[128,64]{1,0:T(8,128)S(1)} %copy.21), kind=kLoop, calls=%fused_computation.5 | loop fusion | flops 3137536 | bytes 131072 | tf_op jit(solution)/shard_map/reduce_sum | solution.py:83
  66.5 0.1 reduce_max.20
  66.6 2.8 %all-to-all-done.1 = f32[4,128,4]{1,2,0:T(4,128)S(1)} async-done(((f32[4,128,4]{1,2,0:T(4,128)}), f32[4,128,4]{1,2,0:T(4,128)S(1)}, u32[]{:S(2)}, u32[]{:S(2)}) %all-to-all-start.1) | async-done | bytes 8224 | tf_op jit(solution)/shard_map/all_to_all | solution.py:98
  69.5 0.1 copy.26
  69.6 0.2 fusion.19
  69.8 0.1 subtract_convert_fusion
  70.0 0.1 slice.9
  70.1 0.1 copy.27
  70.1 7.9 %all_to_all.25 = bf16[4,128,4]{1,2,0:T(4,128)(2,1)S(1)} all-to-all(bf16[4,128,4]{1,2,0:T(4,128)(2,1)S(1)} %copy.28), channel_id=1, replica_groups=mesh['pa'=8,'pb'=4] {'pb'}, dimensions={0} | all-to-all | bytes 8192 | tf_op jit(solution)/shard_map/all_to_all | solution.py:118
  78.1 0.2 copy.34
  78.3 4.5 %fusion.20 = f32[4,128,1,1024]{3,2,1,0:T(1,128)S(1)} fusion(bf16[4,128,4,1]{2,3,1,0:T(2,128)(2,1)S(1)} %copy.34, bf16[4,128,4,1024]{3,2,1,0:T(4,128)(2,1)} %reshape_reshape.3), kind=kOutput, calls=%fused_computation.53 | convolution fusion | flops 4194304 | bytes 6295552 | tf_op jit(solution)/shard_map/sij,sijd->sid/dot_general | solution.py:126
  82.8 1.8 %copy.41 = f32[4,128,1,1024]{3,1,0,2:T(8,128)} copy(f32[4,128,1,1024]{3,2,1,0:T(1,128)S(1)} %fusion.20) | data formatting | bytes 4194304 | tf_op jit(solution)/shard_map/sij,sijd->sid/dot_general | solution.py:126
  84.5 4.4 %all-to-all-start.3 = ((f32[4,128,1024]{2,1,0:T(8,128)}), f32[4,128,1024]{2,1,0:T(8,128)}, u32[]{:S(2)}, u32[]{:S(2)}) async-start(f32[4,128,1024]{2,1,0:T(8,128)} %bitcast.36), calls=%async_computation.3 | async-start | bytes 4194304 | tf_op jit(solution)/shard_map/all_to_all | solution.py:127
  89.0 0.0 reduce-scatter.2.cloned.1.call-start
  89.0 6.7 %mul.94 = f32[4,128,4,1024]{3,2,1,0:T(4,128)} broadcast(bf16[4,128,1024]{2,1,0:T(8,128)(2,1)} %bitcast.38), dimensions={0,1,3} | broadcast | bytes 9437184 | tf_op jit(solution)/shard_map/mul | solution.py:120
  95.8 10.0 %mul.95 = f32[2048,1024]{1,0:T(8,128)} reshape(f32[4,128,4,1024]{3,2,1,0:T(4,128)} %mul.94) | data formatting | bytes 16777216 | tf_op jit(solution)/shard_map/mul | solution.py:120
  105.8 1.8 %fusion.2 = f32[128,1,128]{2,1,0:T(1,128)S(1)} fusion(s32[128,64]{1,0:T(8,128)S(1)} %copy.21, bf16[128,64,1]{1,0,2:T(8,128)(2,1)S(1)} %slice_bitcast_fusion), kind=kOutput, calls=%fused_computation.7 | convolution fusion | flops 3145728 | bytes 114688 | tf_op jit(solution)/shard_map/ic,icr->ir/dot_general | solution.py:107
  107.6 1.1 convolution_multiply_fusion
  108.7 0.0 reduce-scatter.2.cloned.1.call-update
  108.7 0.1 copy.29
  108.8 0.2 mul.92
  109.0 7.9 %convolution_convert_fusion = bf16[512,1024]{1,0:T(8,128)(2,1)} fusion(bf16[1024,1024]{1,0:T(8,128)(2,1)S(1)} %copy-done, f32[2048,1024]{1,0:T(8,128)} %mul.95, f32[2048]{0:T(1024)S(1)} %mul.92, s32[2048]{0:T(1024)S(1)} %bitcast.48), kind=kOutput, calls=%fused_computation.19 | convolution fusion | flops 3227516928 | bytes 11550720 | tf_op jit(solution)/shard_map/dot_general | solution.py:133
  116.9 26.8 %reduce-scatter.2.cloned.1.call-done = f32[16,1024]{1,0:T(8,128)} async-done(((f32[128,1024]{1,0:T(8,128)}), f32[16,1024]{1,0:T(8,128)}) %reduce-scatter.2.cloned.1.call-update) | async-done | bytes 65552 | tf_op jit(solution)/shard_map/reduce_scatter | solution.py:117
  143.7 2.1 %convolution_convert_fusion.2 = bf16[16,1024]{1,0:T(8,128)(2,1)} fusion(bf16[1024,1024]{1,0:T(8,128)(2,1)S(1)} %copy-done, f32[16,1024]{1,0:T(8,128)} %reduce-scatter.2.cloned.1.call-done), kind=kOutput, calls=%fused_computation.27 | convolution fusion | flops 33587200 | bytes 2195456 | tf_op jit(solution)/shard_map/dot_general | solution.py:130
  145.8 0.0 all-to-all-done.3
  145.8 1.8 %reduce_sum.39 = f32[128,1024]{1,0:T(8,128)S(1)} reduce(f32[4,128,1024]{2,1,0:T(8,128)} %all-to-all-done.3, f32[]{:T(128)} %constant.86.clone.1), dimensions={0}, to_apply=%region_5.6 | reduce | flops 393216 | bytes 2621444 | tf_op jit(solution)/shard_map/reduce_sum | solution.py:128
  147.6 0.9 fusion.12
  (18 shorter events, 0.1 us)
Async XLA Ops:
  7.2 1.6 %copy-start = (bf16[1024,1024]{1,0:T(8,128)(2,1)S(1)}, bf16[1024,1024]{1,0:T(8,128)(2,1)}, u32[]{:S(2)}) copy-start(bf16[1024,1024]{1,0:T(8,128)(2,1)} %param.11) | copy-start | bytes 6291460
  9.9 30.2 %collective-permute-start = (bf16[16,1024]{1,0:T(8,128)(2,1)S(1)}, bf16[16,1024]{1,0:T(8,128)(2,1)S(1)}, u32[]{:S(2)}, u32[]{:S(2)}) collective-permute-start(bf16[16,1024]{1,0:T(8,128)(2,1)S(1)} %get-tuple-element.4), channel_id=1, source_target_pairs={{0,4},{4,8},{8,12},{12,16},{16,20},{20,24},{24,28},{28,0},{1,5},{5... | collective-permute-start | bytes 98312 | tf_op jit(solution)/shard_map/ppermute | solution.py:26
  10.4 29.7 %collective-permute-start.1 = (bf16[16,1024]{1,0:T(8,128)(2,1)S(1)}, bf16[16,1024]{1,0:T(8,128)(2,1)S(1)}, u32[]{:S(2)}, u32[]{:S(2)}) collective-permute-start(bf16[16,1024]{1,0:T(8,128)(2,1)S(1)} %get-tuple-element.4), channel_id=1, source_target_pairs={{0,28},{4,0},{8,4},{12,8},{16,12},{20,16},{24,20},{28,24},{1,29},{... | collective-permute-start | bytes 98312 | tf_op jit(solution)/shard_map/ppermute | solution.py:31
  15.0 11.2 %all-to-all-start = ((s32[4,1,512]{2,1,0:T(1,128)}), s32[4,1,512]{2,1,0:T(1,128)S(1)}, u32[]{:S(2)}, u32[]{:S(2)}) async-start(s32[4,1,512]{2,1,0:T(1,128)} %all_to_all.20), calls=%async_computation | async-start | bytes 16384 | tf_op jit(solution)/shard_map/all_to_all | solution.py:91
  20.6 32.5 %all-gather.2.cloned.1.call-start = ((), (), s32[]{:S(2)}) async-start(), calls=%async_computation.5 | async-start | bytes 1310720 | tf_op jit(solution)/shard_map/all_gather | solution.py:92
  32.8 20.0 %copy-start.1 = (bf16[128,1024]{1,0:T(8,128)(2,1)S(1)}, bf16[128,1024]{1,0:T(8,128)(2,1)}, u32[]{:S(2)}) copy-start(bf16[128,1024]{1,0:T(8,128)(2,1)} %param.8) | copy-start | bytes 786436
  40.1 4.2 %collective-permute-start.2 = (bf16[16,1024]{1,0:T(8,128)(2,1)S(1)}, bf16[16,1024]{1,0:T(8,128)(2,1)S(1)}, u32[]{:S(2)}, u32[]{:S(2)}) collective-permute-start(bf16[16,1024]{1,0:T(8,128)(2,1)S(1)} %collective-permute-done), channel_id=1, source_target_pairs={{0,4},{4,8},{8,12},{12,16},{16,20},{20,24},{24,28},{28,0},{1,5},{5... | collective-permute-start | bytes 98312 | tf_op jit(solution)/shard_map/ppermute | solution.py:26
  40.1 4.2 %collective-permute-start.3 = (bf16[16,1024]{1,0:T(8,128)(2,1)S(1)}, bf16[16,1024]{1,0:T(8,128)(2,1)S(1)}, u32[]{:S(2)}, u32[]{:S(2)}) collective-permute-start(bf16[16,1024]{1,0:T(8,128)(2,1)S(1)} %collective-permute-done.1), channel_id=1, source_target_pairs={{0,28},{4,0},{8,4},{12,8},{16,12},{20,16},{24,20},{28,24},{1,29},{... | collective-permute-start | bytes 98312 | tf_op jit(solution)/shard_map/ppermute | solution.py:31
  44.3 4.2 %collective-permute-start.4 = (bf16[16,1024]{1,0:T(8,128)(2,1)S(1)}, bf16[16,1024]{1,0:T(8,128)(2,1)S(1)}, u32[]{:S(2)}, u32[]{:S(2)}) collective-permute-start(bf16[16,1024]{1,0:T(8,128)(2,1)S(1)} %collective-permute-done.2), channel_id=1, source_target_pairs={{0,4},{4,8},{8,12},{12,16},{16,20},{20,24},{24,28},{28,0},{1,5},{5... | collective-permute-start | bytes 98312 | tf_op jit(solution)/shard_map/ppermute | solution.py:26
  44.3 4.6 %collective-permute-start.5 = (bf16[16,1024]{1,0:T(8,128)(2,1)S(1)}, bf16[16,1024]{1,0:T(8,128)(2,1)S(1)}, u32[]{:S(2)}, u32[]{:S(2)}) collective-permute-start(bf16[16,1024]{1,0:T(8,128)(2,1)S(1)} %collective-permute-done.3), channel_id=1, source_target_pairs={{0,28},{4,0},{8,4},{12,8},{16,12},{20,16},{24,20},{28,24},{1,29},{... | collective-permute-start | bytes 98312 | tf_op jit(solution)/shard_map/ppermute | solution.py:31
  48.5 4.2 %collective-permute-start.6 = (bf16[16,1024]{1,0:T(8,128)(2,1)S(1)}, bf16[16,1024]{1,0:T(8,128)(2,1)S(1)}, u32[]{:S(2)}, u32[]{:S(2)}) collective-permute-start(bf16[16,1024]{1,0:T(8,128)(2,1)S(1)} %collective-permute-done.4), channel_id=1, source_target_pairs={{0,4},{4,8},{8,12},{12,16},{16,20},{20,24},{24,28},{28,0},{1,5},{5... | collective-permute-start | bytes 98312 | tf_op jit(solution)/shard_map/ppermute | solution.py:26
  53.2 16.7 %copy-start.2 = (s32[128]{0:T(128)S(1)}, s32[128]{0:T(128)}, u32[]{:S(2)}) copy-start(s32[128]{0:T(128)} %param.14) | copy-start | bytes 1540
  60.7 8.8 %all-to-all-start.1 = ((f32[4,128,4]{1,2,0:T(4,128)}), f32[4,128,4]{1,2,0:T(4,128)S(1)}, u32[]{:S(2)}, u32[]{:S(2)}) async-start(f32[4,128,4]{1,2,0:T(4,128)} %bitcast_multiply_fusion), calls=%async_computation.1 | async-start | bytes 16384 | tf_op jit(solution)/shard_map/all_to_all | solution.py:98
  84.5 61.3 %all-to-all-start.3 = ((f32[4,128,1024]{2,1,0:T(8,128)}), f32[4,128,1024]{2,1,0:T(8,128)}, u32[]{:S(2)}, u32[]{:S(2)}) async-start(f32[4,128,1024]{2,1,0:T(8,128)} %bitcast.36), calls=%async_computation.3 | async-start | bytes 4194304 | tf_op jit(solution)/shard_map/all_to_all | solution.py:127
  89.0 54.7 %reduce-scatter.2.cloned.1.call-start = ((), (), s32[]{:S(2)}) async-start(), calls=%async_computation.6 | async-start | bytes 589824 | tf_op jit(solution)/shard_map/reduce_scatter | solution.py:117
Sparse Core Ops, SparseCore 0:
  23.0 28.5 all-gather.1
  108.8 34.8 reduce-scatter.1
